TPU v7x, 512 devices: a whole 4x8x8 slice. The times are simulated.
512 devices in a mesh: head: 8 (over x, core), blk: 64 (over y, z).
Axes of the slice: x: 4, y: 8, z: 8, core: 2. Of those that a mesh axis runs over, the one named last changes fastest.
Arguments:
- suffix_hidden: bfloat16 [1536, 2048], P('blk'), may hold values from -400 to 400
- prefix_hidden: bfloat16 [16384, 2048], P('blk'), may hold values from -400 to 400
- kv_cache: bfloat16 [2, 16384, 8, 256], P(None, 'blk', 'head'), may hold values from -300 to 300
- norm_gain: float32 [2048], replicated, may hold values from 0.1 to 1.9
- norm_bias: float32 [2048], replicated, may hold values from -3 to 3
- qkv_weight: bfloat16 [2048, 8, 768], P('blk', 'head'), may hold values from -0.125 to 0.125
- qkv_bias: float32 [8, 768], P('head'), may hold values from -3 to 3
- out_weight: bfloat16 [8, 256, 2048], P('head', 'blk'), may hold values from -0.125 to 0.125
- out_bias: float32 [2048], replicated, may hold values from -3 to 3
- suffix_lengths: int32 [4], replicated, may hold values from 1 to 768, 1536 in all
- prefix_blocks: int32 [4], replicated, may hold values from 1 to 32, 64 in all
- block_owner: int32 [64], replicated, may hold values from 0 to 63, each once
- recompute_flag: int32 [16384], P('blk'), may hold values from 0 to 1, as said below
Outputs:
- attn_out: bfloat16 [1536, 2048], P('blk', 'head')
Inputs may be any that keep to these rules, and one draw needn't show every extreme that they name: `recompute_flag`: each storage block of 256 cache rows holds exactly 25 ones.
All inputs are finite; a program needn't handle non-finite values.
Results may differ from a plain program's by a relative error of at most 0.015.
Values may be sent and summed in bfloat16 or wider, within the bound.
A program may use at most 64 MiB of HBM per device.

v0:
```python
import math
import jax
import jax.numpy as jnp
from jax import lax
from jax.sharding import PartitionSpec as P

FLAG_DEV = 25
EPSILON = 1e-05
MASKED = -1e30


def layer_norm(states, norm_scale, norm_shift):
    widened = states.astype(jnp.float32)
    average = jnp.mean(widened, axis=-1, keepdims=True)
    center = widened - average
    variance = jnp.mean(center * center, axis=-1, keepdims=True)
    return (center * lax.rsqrt(variance + EPSILON) * norm_scale + norm_shift).astype(jnp.bfloat16)


def body(
    suffix_hidden,
    prefix_hidden,
    kv_cache,
    norm_gain,
    norm_bias,
    qkv_weight,
    qkv_bias,
    out_weight,
    out_bias,
    suffix_lengths,
    prefix_blocks,
    block_owner,
    recompute_flag,
):
    blk_total = lax.axis_size("blk")
    own_index = lax.axis_index("blk")
    row_count = suffix_hidden.shape[0]
    cache_rows = prefix_hidden.shape[0]
    heads_dev = qkv_weight.shape[1]
    head_dim = qkv_weight.shape[2] // 3
    total_rows = row_count * blk_total
    own_first = own_index * row_count
    tenant_ends = jnp.cumsum(suffix_lengths)
    row_ids = jnp.arange(total_rows, dtype=jnp.int32)
    row_tenant = jnp.sum((row_ids[:, None] >= tenant_ends[None, :]).astype(jnp.int32), axis=1)
    block_ends = jnp.cumsum(prefix_blocks)
    block_slots = jnp.arange(blk_total, dtype=jnp.int32)
    global_block = jnp.sum(jnp.where(block_owner == own_index, block_slots, 0))
    block_tenant = jnp.sum((global_block >= block_ends).astype(jnp.int32))
    normed = layer_norm(suffix_hidden, norm_gain, norm_bias)
    flagged = jnp.argsort(1 - recompute_flag, stable=True)[:FLAG_DEV]
    prefix_normed = layer_norm(prefix_hidden[flagged], norm_gain, norm_bias)
    fetched = lax.all_gather(qkv_weight, "blk", axis=0, tiled=True)
    piece_rows = fetched.shape[0]
    flattened = fetched.reshape(piece_rows, heads_dev * 3 * head_dim)
    kv_part = fetched[:, :, head_dim:].reshape(piece_rows, heads_dev * 2 * head_dim)
    suffix_acc = jnp.dot(normed, flattened, preferred_element_type=jnp.float32)
    prefix_acc = jnp.dot(prefix_normed, kv_part, preferred_element_type=jnp.float32)
    suffix_acc, prefix_acc = (suffix_acc, prefix_acc)
    projected = (
        (suffix_acc + qkv_bias.reshape(-1))
        .astype(jnp.bfloat16)
        .reshape(row_count, heads_dev, 3 * head_dim)
    )
    recomputed = (
        (prefix_acc + qkv_bias[:, head_dim:].reshape(-1))
        .astype(jnp.bfloat16)
        .reshape(FLAG_DEV, heads_dev, 2 * head_dim)
    )
    own_queries = projected[:, :, :head_dim].reshape(row_count, heads_dev * head_dim)
    gathered = lax.all_gather(own_queries, "blk", axis=0, tiled=True)
    prefix_keys = kv_cache[0].at[flagged].set(recomputed[:, :, :head_dim])
    prefix_values = kv_cache[1].at[flagged].set(recomputed[:, :, head_dim:])
    keys_all = jnp.concatenate([prefix_keys, projected[:, :, head_dim : 2 * head_dim]], axis=0)
    values_all = jnp.concatenate([prefix_values, projected[:, :, 2 * head_dim :]], axis=0)
    own_tenant = lax.dynamic_slice_in_dim(row_tenant, own_first, row_count, 0)
    key_tenant = jnp.concatenate([jnp.full((cache_rows,), block_tenant, jnp.int32), own_tenant])
    key_position = jnp.concatenate(
        [jnp.full((cache_rows,), -1, jnp.int32), own_first + jnp.arange(row_count, dtype=jnp.int32)]
    )
    scale = head_dim ** (-0.5)
    qblock = math.gcd(total_rows, 512)
    block_total = total_rows // qblock

    def partial_block(offset):
        query_block = lax.dynamic_slice_in_dim(gathered, offset, qblock, 0).reshape(
            qblock, heads_dev, head_dim
        )
        query_tenant = lax.dynamic_slice_in_dim(row_tenant, offset, qblock, 0)
        query_position = offset + jnp.arange(qblock, dtype=jnp.int32)
        allowed = (query_tenant[:, None] == key_tenant[None, :]) & (
            key_position[None, :] <= query_position[:, None]
        )
        scores = (
            jnp.einsum("qhd,khd->hqk", query_block, keys_all, preferred_element_type=jnp.float32)
            * scale
        )
        gate = allowed[None, :, :]
        row_peak = jnp.max(jnp.where(gate, scores, MASKED), axis=2)
        weights = jnp.where(gate, jnp.exp(scores - row_peak[:, :, None]), 0.0)
        denominator = jnp.sum(weights, axis=2)
        numerator = jnp.einsum(
            "hqk,khd->qhd",
            weights.astype(jnp.bfloat16),
            values_all,
            preferred_element_type=jnp.float32,
        )
        return (numerator.reshape(qblock, heads_dev * head_dim), denominator.T, row_peak.T)

    def fill_block(step_index, buffers):
        numer_buf, denom_buf, peak_buf = buffers
        offset = step_index * qblock
        numerator, denominator, row_peak = partial_block(offset)
        numer_buf = lax.dynamic_update_slice_in_dim(numer_buf, numerator, offset, 0)
        denom_buf = lax.dynamic_update_slice_in_dim(denom_buf, denominator, offset, 0)
        peak_buf = lax.dynamic_update_slice_in_dim(peak_buf, row_peak, offset, 0)
        return (numer_buf, denom_buf, peak_buf)

    initial = (
        jnp.zeros((total_rows, heads_dev * head_dim), jnp.float32),
        jnp.zeros((total_rows, heads_dev), jnp.float32),
        jnp.full((total_rows, heads_dev), MASKED, jnp.float32),
    )
    numer_buf, denom_buf, peak_buf = lax.fori_loop(0, block_total, fill_block, initial)
    numer_view = numer_buf.reshape(blk_total, row_count, heads_dev * head_dim)
    denom_view = denom_buf.reshape(blk_total, row_count, heads_dev)
    peak_view = peak_buf.reshape(blk_total, row_count, heads_dev)
    recv_numer, recv_denom, recv_peak = (
        lax.all_to_all(numer_view, "blk", split_axis=0, concat_axis=0, tiled=True),
        lax.all_to_all(denom_view, "blk", split_axis=0, concat_axis=0, tiled=True),
        lax.all_to_all(peak_view, "blk", split_axis=0, concat_axis=0, tiled=True),
    )
    best = jnp.max(recv_peak, axis=0)
    factor = jnp.exp(recv_peak - best[None])
    summed_denom = jnp.sum(factor * recv_denom, axis=0)
    summed_numer = jnp.sum(
        recv_numer.reshape(blk_total, row_count, heads_dev, head_dim) * factor[:, :, :, None],
        axis=0,
    )
    attended = (summed_numer / summed_denom[:, :, None]).astype(jnp.bfloat16)
    fetched = lax.all_gather(out_weight, "blk", axis=1, tiled=True)
    mixed = jnp.einsum("rhd,hde->re", attended, fetched, preferred_element_type=jnp.float32)
    summed = lax.psum_scatter(
        mixed.astype(jnp.bfloat16), "head", scatter_dimension=1, tiled=True
    ).astype(jnp.float32)
    columns = summed.shape[1]
    bias_part = lax.dynamic_slice_in_dim(out_bias, lax.axis_index("head") * columns, columns, 0)
    return (summed + bias_part).astype(jnp.bfloat16)


def solution(mesh):
    return jax.shard_map(
        body,
        mesh=mesh,
        in_specs=(
            P("blk", None),
            P("blk", None),
            P(None, "blk", "head", None),
            P(),
            P(),
            P("blk", "head", None),
            P("head", None),
            P("head", "blk", None),
            P(),
            P(),
            P(),
            P(),
            P("blk"),
        ),
        out_specs=P("blk", "head"),
        check_vma=False,
    )
```

profile of v0, /device:TPU:8, one launch (start us, length us, event | category | flops | bytes accessed | tf_op | source)
XLA Modules:
  0.0 355.3 jit_solution(12156490804968114255)
XLA Ops:
  6.6 0.7 all-gather.4.cloned.1.call-update
  7.3 0.7 reduce.13
  8.0 0.8 reduce-window.17
  8.8 0.8 reduce-window.18
  9.6 0.7 broadcast_subtract_fusion
  10.3 3.2 sort.17
  13.5 0.6 gather_fusion
  14.2 0.1 convert_reduce_fusion.2
  14.3 0.1 dynamic_slice.20
  14.3 1.3 fusion.58
  15.6 1.3 fusion.59
  16.9 0.7 concatenate.12
  17.6 0.6 concatenate.13
  18.2 1.0 convert_reduce_fusion.1
  19.2 0.1 convert_reduce_fusion
  19.3 1.1 fusion.39
  20.4 0.2 fusion.33
  20.7 1.0 slice_bitcast_fusion.8
  21.7 78.6 %all-gather.4.cloned.1.call-done = bf16[2048,1,768]{2,0,1:T(8,128)(2,1)} async-done(((bf16[32,1,768]{2,0,1:T(8,128)(2,1)}), bf16[2048,1,768]{2,0,1:T(8,128)(2,1)}) %all-gather.4.cloned.1.call-update) | async-done | bytes 3145744 | tf_op jit(solution)/shard_map/all_gather | solution.py:53
  100.3 2.1 fusion.28
  102.4 0.8 scatter_custom_fusion
  103.2 0.8 scatter_custom_fusion.1
  104.0 2.5 fusion.25
  106.5 48.6 %all-gather = bf16[1536,1,256]{2,0,1:T(8,128)(2,1)S(1)} all-gather(bf16[24,1,256]{2,0,1:T(8,128)(2,1)S(1)} %get-tuple-element.211), channel_id=2, replica_groups=mesh['head'=8,'blk'=64] {'blk'}, dimensions={0}, use_global_device_ids=true | all-gather | bytes 798720 | tf_op jit(solution)/shard_map/all_gather | solution.py:71
  155.0 0.7 pad_maximum_fusion
  155.7 0.1 broadcast_in_dim.63
  155.8 0.6 broadcast_in_dim.64
  156.4 0.6 broadcast_in_dim.65
  157.0 11.8 %while.17 = (s32[]{:T(128)}, f32[1536,256]{1,0:T(8,128)S(1)}, f32[1536,1]{0,1:T(1,128)}, f32[1536,1]{0,1:T(1,128)}, s32[1536]{0:T(1024)}, /*index=5*/s32[280]{0:...) while((s32[]{:T(128)}, f32[1536,256]{1,0:T(8,128)S(1)}, ...), condition=%wide.region_15.16_spmd, body=%wide.region_12.15_spmd.sunk | while | flops 149380608 | bytes 2841571 | solution.py:124
  157.0 0.8 dynamic_slice.29
  157.8 1.0 select_reduce_fusion.2
  158.7 1.4 convolution_dynamic-update-slice_fusion.2
  160.1 0.2 fusion.66
  160.3 0.6 constant_dynamic-update-slice_fusion.3
  161.0 0.8 dynamic_slice.29
  161.7 1.0 select_reduce_fusion.2
  162.7 1.4 convolution_dynamic-update-slice_fusion.2
  164.1 0.2 fusion.66
  164.3 0.6 constant_dynamic-update-slice_fusion.3
  164.9 0.8 dynamic_slice.29
  165.7 1.0 select_reduce_fusion.2
  166.6 1.4 convolution_dynamic-update-slice_fusion.2
  168.0 0.2 fusion.66
  168.2 0.6 constant_dynamic-update-slice_fusion.3
  168.8 0.8 reduce.14
  169.6 0.7 reshape.214
  170.3 10.2 %all-to-all-start.1 = ((f32[64,24,1]{1,2,0:T(1,128)}), f32[64,24,1]{1,2,0:T(1,128)S(1)}, u32[]{:S(2)}, u32[]{:S(2)}) async-start(f32[64,24,1]{1,2,0:T(1,128)} %bitcast.20), calls=%async_computation.1 | async-start | bytes 65536 | tf_op jit(solution)/shard_map/all_to_all | solution.py:131
  180.5 0.7 reduce.15
  181.2 0.1 reshape.215
  181.3 10.2 %all-to-all-done.1 = f32[64,24,1]{1,2,0:T(1,128)S(1)} async-done(((f32[64,24,1]{1,2,0:T(1,128)}), f32[64,24,1]{1,2,0:T(1,128)S(1)}, u32[]{:S(2)}, u32[]{:S(2)}) %all-to-all-start.1) | async-done | bytes 6176 | tf_op jit(solution)/shard_map/all_to_all | solution.py:131
  191.5 19.5 %all_to_all.15 = f32[64,24,1]{1,2,0:T(1,128)S(1)} all-to-all(f32[64,24,1]{1,2,0:T(1,128)S(1)} %bitcast.81), channel_id=1, replica_groups=mesh['head'=8,'blk'=64] {'blk'}, dimensions={0} | all-to-all | bytes 12288 | tf_op jit(solution)/shard_map/all_to_all | solution.py:130
  211.0 12.8 %all-to-all-start = ((f32[64,24,256]{2,1,0:T(8,128)}), f32[64,24,256]{2,1,0:T(8,128)S(1)}, u32[]{:S(2)}, u32[]{:S(2)}) async-start(f32[64,24,256]{2,1,0:T(8,128)} %bitcast.74), calls=%async_computation | async-start | bytes 3145728 | tf_op jit(solution)/shard_map/all_to_all | solution.py:129
  223.8 0.0 all-gather.6.cloned.1.call-start
  223.9 0.6 copy.24
  224.5 0.1 all-gather.6.cloned.1.call-update
  224.6 0.1 reduce_max.20
  224.7 0.1 multiply_reduce_fusion.1
  224.8 24.0 %all-to-all-done = f32[64,24,256]{2,1,0:T(8,128)S(1)} async-done(((f32[64,24,256]{2,1,0:T(8,128)}), f32[64,24,256]{2,1,0:T(8,128)S(1)}, u32[]{:S(2)}, u32[]{:S(2)}) %all-to-all-start) | async-done | bytes 1572896 | tf_op jit(solution)/shard_map/all_to_all | solution.py:129
  248.8 0.3 multiply_reduce_fusion
  249.1 62.4 %all-gather.6.cloned.1.call-done = bf16[1,256,2048]{2,0,1:T(2,128)(2,1)} async-done(((bf16[1,4,2048]{2,0,1:T(2,128)(2,1)}), bf16[1,256,2048]{2,0,1:T(2,128)(2,1)}) %all-gather.6.cloned.1.call-update) | async-done | bytes 1048592 | tf_op jit(solution)/shard_map/all_gather | solution.py:141
  311.4 2.9 convolution_convert_fusion
  314.3 0.8 dynamic_slice.21
  315.1 32.3 %reduce-scatter.2.cloned.1.call-done = bf16[24,256]{1,0:T(8,128)(2,1)} async-done(((bf16[24,2048]{1,0:T(8,128)(2,1)}), bf16[24,256]{1,0:T(8,128)(2,1)}) %reduce-scatter.2.cloned.1.call-update) | async-done | bytes 12304 | tf_op jit(solution)/shard_map/reduce_scatter | solution.py:143
  347.4 1.3 add_convert_fusion
  (37 shorter events, 0.2 us)
Async XLA Ops:
  6.5 7.0 %copy-start = (bf16[256,2048]{1,0:T(8,128)(2,1)S(1)}, bf16[256,2048]{1,0:T(8,128)(2,1)}, u32[]{:S(2)}) copy-start(bf16[256,2048]{1,0:T(8,128)(2,1)} %param.16) | copy-start | bytes 3145732
  6.5 93.7 %slice-start = ((f32[1,768]{1,0:T(1,128)}), f32[1,512]{1,0:T(1,128)S(1)}, s32[]{:S(2)}) async-start(f32[1,768]{1,0:T(1,128)} %param.21), calls=%async_computation.7 | async-start | bytes 4096 | tf_op jit(solution)/shard_map/slice | solution.py:66
  6.5 93.7 %copy-start.7 = (f32[2048]{0:T(1024)S(1)}, f32[2048]{0:T(1024)}, u32[]{:S(2)}) copy-start(f32[2048]{0:T(1024)} %param.18) | copy-start | bytes 24580
  6.5 93.7 %copy-start.6 = (f32[2048]{0:T(1024)S(1)}, f32[2048]{0:T(1024)}, u32[]{:S(2)}) copy-start(f32[2048]{0:T(1024)} %param.19) | copy-start | bytes 24580
  6.5 93.7 %all-gather.4.cloned.1.call-start = ((), (), s32[]{:S(2)}) async-start(), calls=%async_computation.4 | async-start | bytes 3194880 | tf_op jit(solution)/shard_map/all_gather | solution.py:53
  14.1 89.8 %copy-start.2 = (bf16[24,2048]{1,0:T(8,128)(2,1)S(1)}, bf16[24,2048]{1,0:T(8,128)(2,1)}, u32[]{:S(2)}) copy-start(bf16[24,2048]{1,0:T(8,128)(2,1)} %param.15) | copy-start | bytes 294916
  14.3 6.4 %copy-start.4 = (s32[1536]{0:T(1024)}, s32[1536]{0:T(1024)S(1)}, u32[]{:S(2)}) copy-start(s32[1536]{0:T(1024)S(1)} %convert_reduce_fusion.2) | copy-start | bytes 18436
  157.0 3.1 copy-start.3
  160.9 3.1 copy-start.3
  164.9 3.1 copy-start.3
  168.8 42.1 %copy-start.1 = (f32[1536,256]{1,0:T(8,128)}, f32[1536,256]{1,0:T(8,128)S(1)}, u32[]{:S(2)}) copy-start(f32[1536,256]{1,0:T(8,128)S(1)} %get-tuple-element.178) | copy-start | bytes 4718596
  168.8 55.0 %copy-start.5 = (bf16[1,4,2048]{2,1,0:T(4,128)(2,1)S(1)}, bf16[1,4,2048]{2,1,0:T(4,128)(2,1)}, u32[]{:S(2)}) copy-start(bf16[1,4,2048]{2,1,0:T(4,128)(2,1)} %param.22) | copy-start | bytes 49156
  170.3 21.2 %all-to-all-start.1 = ((f32[64,24,1]{1,2,0:T(1,128)}), f32[64,24,1]{1,2,0:T(1,128)S(1)}, u32[]{:S(2)}, u32[]{:S(2)}) async-start(f32[64,24,1]{1,2,0:T(1,128)} %bitcast.20), calls=%async_computation.1 | async-start | bytes 65536 | tf_op jit(solution)/shard_map/all_to_all | solution.py:131
  211.0 37.8 %all-to-all-start = ((f32[64,24,256]{2,1,0:T(8,128)}), f32[64,24,256]{2,1,0:T(8,128)S(1)}, u32[]{:S(2)}, u32[]{:S(2)}) async-start(f32[64,24,256]{2,1,0:T(8,128)} %bitcast.74), calls=%async_computation | async-start | bytes 3145728 | tf_op jit(solution)/shard_map/all_to_all | solution.py:129
  223.8 87.6 %all-gather.6.cloned.1.call-start = ((), (), s32[]{:S(2)}) async-start(), calls=%async_computation.5 | async-start | bytes 2129920 | tf_op jit(solution)/shard_map/all_gather | solution.py:141
  224.5 122.9 %reduce-scatter.2.cloned.1.call-start = ((), (), s32[]{:S(2)}) async-start(), calls=%async_computation.6 | async-start | bytes 110592 | tf_op jit(solution)/shard_map/reduce_scatter | solution.py:143
Sparse Core Ops, SparseCore 0:
  10.4 89.7 all-gather.3
  227.7 83.7 all-gather.5
  314.5 32.9 reduce-scatter.1
where the time goes:
time: 356 us; the launch traced here: 355 us
  waiting for transfers between devices  208 us (58%)
  blocking collectives  68 us (19%)
  starting transfers between devices  23.1 us (6%)
  other arithmetic  15.8 us (4%)
  matrix products  14.5 us (4%)
  between operations  13.3 us (4%)
  local copies, waits for them, and re-layouts  12.2 us (3%)
    all_gather x1, waiting for transfers between devices, body(): fetched = lax.all_gather(qkv_weight, 'blk', axis=0, tiled=True)  78.6 us
    all_gather x1, waiting for transfers between devices, body(): fetched = lax.all_gather(out_weight, 'blk', axis=1, tiled=True)  62.4 us
    all_gather x1, blocking collectives, body(): gathered = lax.all_gather(own_queries, 'blk', axis=0, tiled=True)  48.6 us
    reduce_scatter x1, waiting for transfers between devices, body(): lax.psum_scatter(mixed.astype(jnp.bfloat16), 'head', scatter_dimension=1,...  32.3 us
    all_to_all x1, waiting for transfers between devices, body(): lax.all_to_all(numer_view, 'blk', split_axis=0, concat_axis=0, tiled=True)  24 us
    all_to_all x1, blocking collectives, body(): lax.all_to_all(denom_view, 'blk', split_axis=0, concat_axis=0, tiled=True)  19.5 us
    all_to_all x1, starting transfers between devices, body(): lax.all_to_all(numer_view, 'blk', split_axis=0, concat_axis=0, tiled=True)  12.8 us
    all_to_all x1, waiting for transfers between devices, body(): lax.all_to_all(peak_view, 'blk', split_axis=0, concat_axis=0, tiled=True)  10.2 us
  transfers between devices with their start and end apart: 5, of which 5 were waited for; matrix products, arithmetic and copies ran while one was open for 5% of the time, Pallas kernels for 0%

commit v1 on v0

--- a/solution.py
+++ b/solution.py
@@ -7,6 +7,14 @@
 FLAG_DEV = 25
 EPSILON = 1e-05
 MASKED = -1e30
+
+
+def gather_by_exchange(shard, axis, dim):
+    size = lax.axis_size(axis)
+    repeats = [size if d == dim else 1 for d in range(shard.ndim)]
+    return lax.all_to_all(
+        jnp.tile(shard, repeats), axis, split_axis=dim, concat_axis=dim, tiled=True
+    )
 
 
 def layer_norm(states, norm_scale, norm_shift):
@@ -68,7 +76,7 @@
         .reshape(FLAG_DEV, heads_dev, 2 * head_dim)
     )
     own_queries = projected[:, :, :head_dim].reshape(row_count, heads_dev * head_dim)
-    gathered = lax.all_gather(own_queries, "blk", axis=0, tiled=True)
+    gathered = gather_by_exchange(own_queries, "blk", 0)
     prefix_keys = kv_cache[0].at[flagged].set(recomputed[:, :, :head_dim])
     prefix_values = kv_cache[1].at[flagged].set(recomputed[:, :, head_dim:])
     keys_all = jnp.concatenate([prefix_keys, projected[:, :, head_dim : 2 * head_dim]], axis=0)

time: 356 us -> 324 us (0.910)
  blocking collectives: 68 us -> 15.7 us
  waiting for transfers between devices: 208 us -> 230 us
    all_gather x1 -> x0, blocking collectives: 48.6 us -> none  [body(): gathered = lax.all_gather(own_queries, 'blk', axis=0, tiled=True)]
    all_to_all x1, waiting for transfers between devices: 24 us -> 35.8 us  [body(): lax.all_to_all(numer_view, 'blk', split_axis=0, concat_axis=0, tiled=True)]
    all_to_all x0 -> x1, waiting for transfers between devices: none -> 11.5 us  [gather_by_exchange(): lax.all_to_all(jnp.tile(shard, repeats), axis, split_axis=dim, concat_axi...]
    all_to_all x0 -> x1, starting transfers between devices: none -> 9.24 us  [gather_by_exchange(): lax.all_to_all(jnp.tile(shard, repeats), axis, split_axis=dim, concat_axi...]
    all_to_all x1, starting transfers between devices: 12.8 us -> 5.56 us  [body(): lax.all_to_all(numer_view, 'blk', split_axis=0, concat_axis=0, tiled=True)]
    all_gather x1, waiting for transfers between devices: 62.4 us -> 55.5 us  [body(): fetched = lax.all_gather(out_weight, 'blk', axis=1, tiled=True)]
    all_gather x1, waiting for transfers between devices: 78.6 us -> 84 us  [body(): fetched = lax.all_gather(qkv_weight, 'blk', axis=0, tiled=True)]
    all_to_all x1, blocking collectives: 19.5 us -> 15.7 us  [body(): lax.all_to_all(denom_view, 'blk', split_axis=0, concat_axis=0, tiled=True)]
  transfers between devices with their start and end apart: 5 -> 6, of which waited for: 5 -> 6; matrix products, arithmetic and copies ran while one was open for 5% -> 6% of each run, Pallas kernels for 0% -> 0%
where the time goes in v1:
time: 324 us; the launch traced here: 323 us
  waiting for transfers between devices  230 us (71%)
  starting transfers between devices  21.7 us (7%)
  blocking collectives  15.7 us (5%)
  other arithmetic  15.2 us (5%)
  matrix products  14.6 us (5%)
  between operations  13.4 us (4%)
  local copies, waits for them, and re-layouts  12.1 us (4%)
    all_gather x1, waiting for transfers between devices, body(): fetched = lax.all_gather(qkv_weight, 'blk', axis=0, tiled=True)  84 us
    all_gather x1, waiting for transfers between devices, body(): fetched = lax.all_gather(out_weight, 'blk', axis=1, tiled=True)  55.5 us
    all_to_all x1, waiting for transfers between devices, body(): lax.all_to_all(numer_view, 'blk', split_axis=0, concat_axis=0, tiled=True)  35.8 us
    reduce_scatter x1, waiting for transfers between devices, body(): lax.psum_scatter(mixed.astype(jnp.bfloat16), 'head', scatter_dimension=1,...  32.3 us
    all_to_all x1, blocking collectives, body(): lax.all_to_all(denom_view, 'blk', split_axis=0, concat_axis=0, tiled=True)  15.7 us
    all_to_all x1, waiting for transfers between devices, gather_by_exchange(): lax.all_to_all(jnp.tile(shard, repeats), axis, split_axis=dim, concat_axi...  11.5 us
    all_to_all x1, waiting for transfers between devices, body(): lax.all_to_all(peak_view, 'blk', split_axis=0, concat_axis=0, tiled=True)  10.2 us
    all_to_all x1, starting transfers between devices, gather_by_exchange(): lax.all_to_all(jnp.tile(shard, repeats), axis, split_axis=dim, concat_axi...  9.24 us
  transfers between devices with their start and end apart: 6, of which 6 were waited for; matrix products, arithmetic and copies ran while one was open for 6% of the time, Pallas kernels for 0%

profile of v1, /device:TPU:8, one launch (start us, length us, event | category | flops | bytes accessed | tf_op | source)
XLA Modules:
  0.0 322.9 jit_solution(11943088617724902616)
XLA Ops:
  6.5 0.7 all-gather.3.cloned.1.call-update
  7.3 0.7 broadcast_subtract_fusion
  7.9 3.2 sort.17
  11.1 0.7 reduce.13
  11.8 0.8 reduce-window.17
  12.6 1.3 fusion.58
  14.0 0.1 convert_reduce_fusion.2
  14.1 1.0 convert_reduce_fusion.1
  15.1 1.1 fusion.39
  16.2 84.0 %all-gather.3.cloned.1.call-done = bf16[2048,1,768]{2,0,1:T(8,128)(2,1)} async-done(((bf16[32,1,768]{2,0,1:T(8,128)(2,1)}), bf16[2048,1,768]{2,0,1:T(8,128)(2,1)}) %all-gather.3.cloned.1.call-update) | async-done | bytes 3145744 | tf_op jit(solution)/shard_map/all_gather | solution.py:61
  100.2 2.6 fusion.25
  102.9 0.9 tile.9
  103.8 9.2 %all-to-all-start = ((bf16[64,24,256]{2,1,0:T(8,128)(2,1)}), bf16[64,24,256]{2,1,0:T(8,128)(2,1)S(1)}, u32[]{:S(2)}, u32[]{:S(2)}) async-start(bf16[64,24,256]{2,1,0:T(8,128)(2,1)} %tile.9), calls=%async_computation | async-start | bytes 1572864 | tf_op jit(solution)/shard_map/all_to_all | solution.py:15
  113.1 0.2 reduce-window.18
  113.2 0.6 gather_fusion
  113.9 0.1 dynamic_slice.20
  114.0 1.3 fusion.59
  115.3 0.6 concatenate.12
  115.9 0.6 concatenate.13
  116.5 0.1 convert_reduce_fusion
  116.6 0.2 fusion.33
  116.9 2.1 fusion.28
  119.0 0.8 scatter_custom_fusion
  119.8 0.8 scatter_custom_fusion.1
  120.6 0.7 pad_maximum_fusion
  121.3 11.5 %all-to-all-done = bf16[64,24,256]{2,1,0:T(8,128)(2,1)S(1)} async-done(((bf16[64,24,256]{2,1,0:T(8,128)(2,1)}), bf16[64,24,256]{2,1,0:T(8,128)(2,1)S(1)}, u32[]{:S(2)}, u32[]{:S(2)}) %all-to-all-start) | async-done | bytes 786464 | tf_op jit(solution)/shard_map/all_to_all | solution.py:15
  132.8 0.1 broadcast_in_dim.63
  132.9 0.6 broadcast_in_dim.64
  133.5 0.6 broadcast_in_dim.65
  134.1 11.8 %while.17 = (s32[]{:T(128)}, f32[1536,256]{1,0:T(8,128)S(1)}, f32[1536,1]{0,1:T(1,128)}, f32[1536,1]{0,1:T(1,128)}, s32[1536]{0:T(1024)}, /*index=5*/s32[280]{0:...) while((s32[]{:T(128)}, f32[1536,256]{1,0:T(8,128)S(1)}, ...), condition=%wide.region_15.16_spmd, body=%wide.region_12.15_spmd.sunk | while | flops 149380608 | bytes 2841571 | solution.py:132
  134.1 0.8 dynamic_slice.29
  134.8 1.0 select_reduce_fusion.2
  135.8 1.4 convolution_dynamic-update-slice_fusion.2
  137.2 0.2 fusion.66
  137.4 0.6 constant_dynamic-update-slice_fusion.3
  138.0 0.8 dynamic_slice.29
  138.8 1.0 select_reduce_fusion.2
  139.7 1.4 convolution_dynamic-update-slice_fusion.2
  141.1 0.2 fusion.66
  141.3 0.6 constant_dynamic-update-slice_fusion.3
  141.9 0.8 dynamic_slice.29
  142.7 1.0 select_reduce_fusion.2
  143.7 1.4 convolution_dynamic-update-slice_fusion.2
  145.1 0.2 fusion.66
  145.3 0.6 constant_dynamic-update-slice_fusion.3
  145.9 0.8 reduce.14
  146.7 0.7 reshape.217
  147.3 6.8 %all-to-all-start.2 = ((f32[64,24,1]{1,2,0:T(1,128)}), f32[64,24,1]{1,2,0:T(1,128)S(1)}, u32[]{:S(2)}, u32[]{:S(2)}) async-start(f32[64,24,1]{1,2,0:T(1,128)} %bitcast.21), calls=%async_computation.2 | async-start | bytes 65536 | tf_op jit(solution)/shard_map/all_to_all | solution.py:139
  154.2 0.7 reduce.15
  154.9 0.1 reshape.218
  155.0 10.2 %all-to-all-done.2 = f32[64,24,1]{1,2,0:T(1,128)S(1)} async-done(((f32[64,24,1]{1,2,0:T(1,128)}), f32[64,24,1]{1,2,0:T(1,128)S(1)}, u32[]{:S(2)}, u32[]{:S(2)}) %all-to-all-start.2) | async-done | bytes 6176 | tf_op jit(solution)/shard_map/all_to_all | solution.py:139
  165.2 15.7 %all_to_all.24 = f32[64,24,1]{1,2,0:T(1,128)S(1)} all-to-all(f32[64,24,1]{1,2,0:T(1,128)S(1)} %bitcast.83), channel_id=1, replica_groups=mesh['head'=8,'blk'=64] {'blk'}, dimensions={0} | all-to-all | bytes 12288 | tf_op jit(solution)/shard_map/all_to_all | solution.py:138
  181.0 5.6 %all-to-all-start.1 = ((f32[64,24,256]{2,1,0:T(8,128)}), f32[64,24,256]{2,1,0:T(8,128)S(1)}, u32[]{:S(2)}, u32[]{:S(2)}) async-start(f32[64,24,256]{2,1,0:T(8,128)} %bitcast.76), calls=%async_computation.1 | async-start | bytes 3145728 | tf_op jit(solution)/shard_map/all_to_all | solution.py:137
  186.6 0.6 copy.24
  187.2 0.1 all-gather.5.cloned.1.call-update
  187.3 0.1 reduce_max.20
  187.4 0.1 multiply_reduce_fusion.1
  187.5 35.8 %all-to-all-done.1 = f32[64,24,256]{2,1,0:T(8,128)S(1)} async-done(((f32[64,24,256]{2,1,0:T(8,128)}), f32[64,24,256]{2,1,0:T(8,128)S(1)}, u32[]{:S(2)}, u32[]{:S(2)}) %all-to-all-start.1) | async-done | bytes 1572896 | tf_op jit(solution)/shard_map/all_to_all | solution.py:137
  223.3 0.3 multiply_reduce_fusion
  223.6 55.5 %all-gather.5.cloned.1.call-done = bf16[1,256,2048]{2,0,1:T(2,128)(2,1)} async-done(((bf16[1,4,2048]{2,0,1:T(2,128)(2,1)}), bf16[1,256,2048]{2,0,1:T(2,128)(2,1)}) %all-gather.5.cloned.1.call-update) | async-done | bytes 1048592 | tf_op jit(solution)/shard_map/all_gather | solution.py:149
  279.0 2.9 convolution_convert_fusion
  281.9 0.8 dynamic_slice.21
  282.7 32.3 %reduce-scatter.2.cloned.1.call-done = bf16[24,256]{1,0:T(8,128)(2,1)} async-done(((bf16[24,2048]{1,0:T(8,128)(2,1)}), bf16[24,256]{1,0:T(8,128)(2,1)}) %reduce-scatter.2.cloned.1.call-update) | async-done | bytes 12304 | tf_op jit(solution)/shard_map/reduce_scatter | solution.py:151
  315.0 1.3 add_convert_fusion
  (41 shorter events, 0.2 us)
Async XLA Ops:
  6.5 106.7 %copy-start = (bf16[256,2048]{1,0:T(8,128)(2,1)S(1)}, bf16[256,2048]{1,0:T(8,128)(2,1)}, u32[]{:S(2)}) copy-start(bf16[256,2048]{1,0:T(8,128)(2,1)} %param.16) | copy-start | bytes 3145732
  6.5 93.7 %all-gather.3.cloned.1.call-start = ((), (), s32[]{:S(2)}) async-start(), calls=%async_computation.5 | async-start | bytes 3194880 | tf_op jit(solution)/shard_map/all_gather | solution.py:61
  14.1 99.8 %copy-start.4 = (s32[1536]{0:T(1024)}, s32[1536]{0:T(1024)S(1)}, u32[]{:S(2)}) copy-start(s32[1536]{0:T(1024)S(1)} %convert_reduce_fusion.2) | copy-start | bytes 18436
  16.2 96.8 %copy-start.8 = (s32[4]{0:T(128)S(1)}, s32[4]{0:T(128)}, u32[]{:S(2)}) copy-start(s32[4]{0:T(128)} %param.25) | copy-start | bytes 52
  102.8 14.1 %copy-start.2 = (bf16[2,256,1,256]{3,1,2,0:T(8,128)(2,1)S(1)}, bf16[2,256,1,256]{3,1,2,0:T(8,128)(2,1)}, u32[]{:S(2)}) copy-start(bf16[2,256,1,256]{3,1,2,0:T(8,128)(2,1)} %param.17) | copy-start | bytes 786436
  102.8 14.1 %slice-start = ((f32[1,768]{1,0:T(1,128)}), f32[1,512]{1,0:T(1,128)S(1)}, s32[]{:S(2)}) async-start(f32[1,768]{1,0:T(1,128)} %param.21), calls=%async_computation.8 | async-start | bytes 4096 | tf_op jit(solution)/shard_map/slice | solution.py:74
  102.8 14.1 %copy-start.6 = (f32[2048]{0:T(1024)S(1)}, f32[2048]{0:T(1024)}, u32[]{:S(2)}) copy-start(f32[2048]{0:T(1024)} %param.19) | copy-start | bytes 24580
  102.8 14.1 %copy-start.7 = (f32[2048]{0:T(1024)S(1)}, f32[2048]{0:T(1024)}, u32[]{:S(2)}) copy-start(f32[2048]{0:T(1024)} %param.18) | copy-start | bytes 24580
  103.8 29.0 %all-to-all-start = ((bf16[64,24,256]{2,1,0:T(8,128)(2,1)}), bf16[64,24,256]{2,1,0:T(8,128)(2,1)S(1)}, u32[]{:S(2)}, u32[]{:S(2)}) async-start(bf16[64,24,256]{2,1,0:T(8,128)(2,1)} %tile.9), calls=%async_computation | async-start | bytes 1572864 | tf_op jit(solution)/shard_map/all_to_all | solution.py:15
  134.1 3.1 copy-start.3
  138.0 3.1 copy-start.3
  141.9 3.1 copy-start.3
  145.9 35.1 %copy-start.1 = (f32[1536,256]{1,0:T(8,128)}, f32[1536,256]{1,0:T(8,128)S(1)}, u32[]{:S(2)}) copy-start(f32[1536,256]{1,0:T(8,128)S(1)} %get-tuple-element.178) | copy-start | bytes 4718596
  145.9 40.7 %copy-start.5 = (bf16[1,4,2048]{2,1,0:T(4,128)(2,1)S(1)}, bf16[1,4,2048]{2,1,0:T(4,128)(2,1)}, u32[]{:S(2)}) copy-start(bf16[1,4,2048]{2,1,0:T(4,128)(2,1)} %param.22) | copy-start | bytes 49156
  147.3 17.9 %all-to-all-start.2 = ((f32[64,24,1]{1,2,0:T(1,128)}), f32[64,24,1]{1,2,0:T(1,128)S(1)}, u32[]{:S(2)}, u32[]{:S(2)}) async-start(f32[64,24,1]{1,2,0:T(1,128)} %bitcast.21), calls=%async_computation.2 | async-start | bytes 65536 | tf_op jit(solution)/shard_map/all_to_all | solution.py:139
  181.0 42.3 %all-to-all-start.1 = ((f32[64,24,256]{2,1,0:T(8,128)}), f32[64,24,256]{2,1,0:T(8,128)S(1)}, u32[]{:S(2)}, u32[]{:S(2)}) async-start(f32[64,24,256]{2,1,0:T(8,128)} %bitcast.76), calls=%async_computation.1 | async-start | bytes 3145728 | tf_op jit(solution)/shard_map/all_to_all | solution.py:137
  186.5 92.5 %all-gather.5.cloned.1.call-start = ((), (), s32[]{:S(2)}) async-start(), calls=%async_computation.6 | async-start | bytes 2129920 | tf_op jit(solution)/shard_map/all_gather | solution.py:149
  187.3 127.8 %reduce-scatter.2.cloned.1.call-start = ((), (), s32[]{:S(2)}) async-start(), calls=%async_computation.7 | async-start | bytes 110592 | tf_op jit(solution)/shard_map/reduce_scatter | solution.py:151
Sparse Core Ops, SparseCore 0:
  10.4 89.7 all-gather.2
  190.4 88.5 all-gather.4
  282.1 32.9 reduce-scatter.1
